TPU v7x, 32 devices: a whole 2x2x4 slice. The times are simulated.
32 devices in a mesh: role: 2 (over y), tile: 16 (over z, x, core).
Axes of the slice: x: 2, y: 2, z: 4, core: 2. Of those that a mesh axis runs over, the one named last changes fastest.
Arguments:
- fields_pair: float32 [2, 512, 16384], P('role', None, 'tile'), may hold values from 0 to 1
- velocity: float32 [16384], P('tile'), may hold values from -0.5 to 0.5
- growth: float32 [16384], P('tile'), may hold values from 0.05 to 0.5
- features: bfloat16 [512, 1024], replicated, may hold values from -6 to 6
- assignment: int32 [512], replicated, may hold values from 0 to 511, each once
- out_pair: float32 [2, 1024, 16384], P('role', None, 'tile'), may hold values from -0.1875 to 0.1875
- hidden_pair: float32 [2, 5, 1024, 1024], P('role', None, 'tile'), may hold values from -0.1875 to 0.1875
Outputs:
- fields_next: float32 [2, 512, 16384], P('role', None, 'tile')
- out_next: float32 [2, 1024, 16384], P('role', None, 'tile')
- hidden_next: float32 [2, 5, 1024, 1024], P('role', None, 'tile')
Inputs may be any that keep to these rules, and one draw needn't show every extreme that they name: `assignment`: a permutation of the 512 members.
All inputs are finite; a program needn't handle non-finite values.
Results may differ from a plain program's by a relative error of at most 0.0022.
The roundings to bfloat16 on the way count: a program that leaves them out, or rounds other values in their place, can miss the bound.
Values may be sent and summed in bfloat16 or wider, within the bound.
A program may use at most 192 MiB of HBM per device.

v0:
```python
import jax
import jax.numpy as jnp
from jax import lax
from jax.sharding import PartitionSpec as P

momentum_decay = 0.9
step_size = 0.1


def extended(value, axis, dim, width):
    count, length = (lax.axis_size(axis), value.shape[dim])
    up = [(i, (i + 1) % count) for i in range(count)]
    down = [(j, i) for i, j in up]
    last = lax.slice_in_dim(value, length - width, length, axis=dim)
    leading = lax.slice_in_dim(value, 0, width, axis=dim)
    before = lax.ppermute(last, axis, up)
    after = lax.ppermute(leading, axis, down)
    return jnp.concatenate([before, value, after], axis=dim)


def silu_slope(values):
    logistic = jax.nn.sigmoid(values)
    return logistic * (1.0 + values * (1.0 - logistic))


def advance(padded, growth):
    states = padded[:-1]
    velocity_row = padded[-1]
    outflow = (
        jnp.maximum(velocity_row[:-1], 0.0) * states[:, :-1]
        + jnp.minimum(velocity_row[:-1], 0.0) * states[:, 1:]
    )
    carried = states[:, 1:-1] - outflow[:, 1:] + outflow[:, :-1]
    return carried + growth * carried * (1.0 - carried)


def to_trainer(value):
    return lax.ppermute(value.astype(jnp.bfloat16), "role", [(0, 1)])


def to_solver(value):
    return lax.ppermute(value.astype(jnp.bfloat16), "role", [(1, 0)])


def plain_training(features, hidden_narrow, out_narrow, own_fields, own_out, own_hidden):
    layer_count, unit_rows = own_hidden.shape[:2]
    batch = own_fields.shape[0]
    first_unit = lax.axis_index("tile") * unit_rows
    momentum_out = to_trainer(own_out)
    momentum_hidden = to_trainer(own_hidden)
    full_hidden = [
        lax.all_gather(hidden_narrow[i], "tile", axis=0, tiled=True) for i in range(layer_count)
    ]
    inputs, summed_list = ([], [])
    activation = features
    for i in range(layer_count):
        inputs.append(activation)
        summed = jnp.dot(activation, full_hidden[i], preferred_element_type=jnp.float32)
        summed_list.append(summed)
        activation = jax.nn.silu(summed).astype(jnp.bfloat16)
    predicted = jnp.dot(activation, out_narrow, preferred_element_type=jnp.float32)
    residual = ((predicted - own_fields) / batch).astype(jnp.bfloat16)
    partial_grad = lax.dot_general(
        residual, out_narrow, (((1,), (1,)), ((), ())), preferred_element_type=jnp.float32
    )
    upstream = lax.psum(partial_grad, "tile")
    grad_out = jnp.dot(activation.T, residual, preferred_element_type=jnp.float32)
    sent_out = to_solver(grad_out)
    gradients, sent = ([], [])
    for i in reversed(range(layer_count)):
        slope = (upstream * silu_slope(summed_list[i])).astype(jnp.bfloat16)
        own_inputs = lax.dynamic_slice_in_dim(inputs[i], first_unit, unit_rows, 1)
        gradient = jnp.dot(own_inputs.T, slope, preferred_element_type=jnp.float32)
        gradients.append(gradient)
        sent.append(to_solver(gradient))
        if i > 0:
            upstream = lax.dot_general(
                slope, full_hidden[i], (((1,), (1,)), ((), ())), preferred_element_type=jnp.float32
            )
    solver_side = lax.axis_index("role") == 0
    other_out = jnp.where(solver_side, sent_out, momentum_out)
    other_hidden = jnp.where(solver_side, jnp.stack(sent[::-1]), momentum_hidden)
    return (grad_out, jnp.stack(gradients[::-1]), other_out, other_hidden)


def body(fields_pair, velocity, growth, features, assignment, out_pair, hidden_pair):
    solver_side = lax.axis_index("role") == 0
    own_fields = fields_pair[0]
    own_out = out_pair[0]
    own_hidden = hidden_pair[0]
    stacked = jnp.concatenate([own_fields, velocity[None, :]], axis=0)
    advanced = advance(extended(stacked, "tile", 1, 1), growth)
    fresh_fields = to_trainer(advanced)
    grad_out, grad_hidden, other_out, other_hidden = plain_training(
        features,
        own_hidden.astype(jnp.bfloat16),
        own_out.astype(jnp.bfloat16),
        own_fields,
        own_out,
        own_hidden,
    )
    grad_out, grad_hidden, other_out, other_hidden = (
        v.astype(jnp.float32) for v in (grad_out, grad_hidden, other_out, other_hidden)
    )
    out_next = jnp.where(
        solver_side,
        momentum_decay * own_out + other_out,
        own_out - step_size * (momentum_decay * other_out + grad_out),
    )
    hidden_next = jnp.where(
        solver_side,
        momentum_decay * own_hidden + other_hidden,
        own_hidden - step_size * (momentum_decay * other_hidden + grad_hidden),
    )
    next_batch = jnp.take(fresh_fields, assignment, axis=0).astype(jnp.float32)
    fields_next = jnp.where(solver_side, advanced, next_batch)
    return (fields_next[None], out_next[None], hidden_next[None])


def solution(mesh):
    return jax.shard_map(
        body,
        mesh=mesh,
        in_specs=(
            P("role", None, "tile"),
            P("tile"),
            P("tile"),
            P(),
            P(),
            P("role", None, "tile"),
            P("role", None, "tile", None),
        ),
        out_specs=(P("role", None, "tile"), P("role", None, "tile"), P("role", None, "tile", None)),
        check_vma=False,
    )
```

profile of v0, /device:TPU:0, one launch (start us, length us, event | category | flops | bytes accessed | tf_op | source)
XLA Modules:
  0.0 390.6 jit_solution(13564146009136946338)
XLA Ops:
  13.1 5.9 %collective-permute-start.10 = (bf16[5,64,1024]{2,1,0:T(8,128)(2,1)}, bf16[5,64,1024]{2,1,0:T(8,128)(2,1)}, u32[]{:S(2)}, u32[]{:S(2)}) collective-permute-start(bf16[5,64,1024]{2,1,0:T(8,128)(2,1)} %copy-done.6), channel_id=1, source_target_pairs={{0,16},{1,17},{2,18},{3,19},{4,20},{5,21},{6,22},{7,23},{8,24},{9,... | collective-permute-start | bytes 1966088 | tf_op jit(solution)/shard_map/ppermute | solution.py:38
  19.0 4.0 %bitcast_convert_fusion = bf16[1024,1024]{1,0:T(8,128)(2,1)} fusion(f32[1,1024,1024]{2,1,0:T(8,128)} %param.12), kind=kLoop, calls=%fused_computation.8 | loop fusion | flops 1048576 | bytes 6291456 | tf_op jit(solution)/shard_map/convert_element_type | solution.py:97
  23.0 2.8 collective-permute-start.4
  26.0 4.4 %collective-permute-start.1 = (f32[513,1]{1,0:T(8,128)S(1)}, f32[513,1]{1,0:T(8,128)S(1)}, u32[]{:S(2)}, u32[]{:S(2)}) collective-permute-start(f32[513,1]{1,0:T(8,128)S(1)} %get-tuple-element.8), channel_id=1, source_target_pairs={{1,0},{2,1},{3,2},{4,3},{5,4},{6,5},{7,6},{8,7},{9,8},{10,9},{11,1... | collective-permute-start | bytes 6164 | tf_op jit(solution)/shard_map/ppermute | solution.py:17
  30.4 5.4 %collective-permute-done = f32[513,1]{1,0:T(8,128)S(1)} collective-permute-done((f32[513,1]{1,0:T(8,128)S(1)}, f32[513,1]{1,0:T(8,128)S(1)}, u32[]{:S(2)}, u32[]{:S(2)}) %collective-permute-start) | collective-permute-done | bytes 2084 | tf_op jit(solution)/shard_map/ppermute | solution.py:16
  36.7 2.4 fusion.59
  40.6 15.2 %all-gather.11.cloned.1.call-done = bf16[1,1024,1024]{2,1,0:T(8,128)(2,1)} async-done(((bf16[1,64,1024]{2,1,0:T(8,128)(2,1)}), bf16[1,1024,1024]{2,1,0:T(8,128)(2,1)}) %all-gather.11.cloned.1.call-update) | async-done | bytes 2097168 | tf_op jit(solution)/shard_map/all_gather | solution.py:52
  55.8 4.6 %multiply_convert_fusion.10 = (bf16[512,1024]{1,0:T(8,128)(2,1)}, f32[512,1024]{1,0:T(8,128)}) fusion(bf16[512,1024]{1,0:T(8,128)(2,1)S(1)} %copy-done, bf16[1,1024,1024]{2,1,0:T(8,128)(2,1)} %all-gather.11.cloned.1.call-done), kind=kOutput, calls=%fused_computation.51 | convolution fusion | flops 1076363264 | bytes 6291456 | tf_op jit(solution)/shard_map/dot_general | solution.py:58
  60.5 37.8 %all-gather.13.cloned.1.call-done = bf16[1,1024,1024]{2,1,0:T(8,128)(2,1)} async-done(((bf16[1,64,1024]{2,1,0:T(8,128)(2,1)}), bf16[1,1024,1024]{2,1,0:T(8,128)(2,1)}) %all-gather.13.cloned.1.call-update) | async-done | bytes 2097168 | tf_op jit(solution)/shard_map/all_gather | solution.py:52
  98.2 4.7 %multiply_convert_fusion.9 = (bf16[512,1024]{1,0:T(8,128)(2,1)S(1)}, f32[512,1024]{1,0:T(8,128)}) fusion(bf16[512,1024]{1,0:T(8,128)(2,1)} %get-tuple-element.14, bf16[1,1024,1024]{2,1,0:T(8,128)(2,1)} %all-gather.13.cloned.1.call-done), kind=kOutput, calls=%fused_computation.49 | convolution fusion | flops 1076363264 | bytes 6291456 | tf_op jit(solution)/shard_map/dot_general | solution.py:58
  102.9 37.7 %all-gather.15.cloned.1.call-done = bf16[1,1024,1024]{2,1,0:T(8,128)(2,1)} async-done(((bf16[1,64,1024]{2,1,0:T(8,128)(2,1)}), bf16[1,1024,1024]{2,1,0:T(8,128)(2,1)}) %all-gather.15.cloned.1.call-update) | async-done | bytes 2097168 | tf_op jit(solution)/shard_map/all_gather | solution.py:52
  140.6 4.7 %multiply_convert_fusion.8 = (bf16[512,1024]{1,0:T(8,128)(2,1)}, f32[512,1024]{1,0:T(8,128)}) fusion(bf16[512,1024]{1,0:T(8,128)(2,1)S(1)} %get-tuple-element.16, bf16[1,1024,1024]{2,1,0:T(8,128)(2,1)} %all-gather.15.cloned.1.call-done), kind=kOutput, calls=%fused_computation.47 | convolution fusion | flops 1076363264 | bytes 6291456 | tf_op jit(solution)/shard_map/dot_general | solution.py:58
  145.3 37.5 %all-gather.17.cloned.1.call-done = bf16[1,1024,1024]{2,1,0:T(8,128)(2,1)} async-done(((bf16[1,64,1024]{2,1,0:T(8,128)(2,1)}), bf16[1,1024,1024]{2,1,0:T(8,128)(2,1)}) %all-gather.17.cloned.1.call-update) | async-done | bytes 2097168 | tf_op jit(solution)/shard_map/all_gather | solution.py:52
  182.8 4.7 %multiply_convert_fusion.7 = (bf16[512,1024]{1,0:T(8,128)(2,1)S(1)}, f32[512,1024]{1,0:T(8,128)}) fusion(bf16[512,1024]{1,0:T(8,128)(2,1)} %get-tuple-element.18, bf16[1,1024,1024]{2,1,0:T(8,128)(2,1)} %all-gather.17.cloned.1.call-done), kind=kOutput, calls=%fused_computation.45 | convolution fusion | flops 1076363264 | bytes 6291456 | tf_op jit(solution)/shard_map/dot_general | solution.py:58
  187.6 38.1 %all-gather.19.cloned.1.call-done = bf16[1,1024,1024]{2,1,0:T(8,128)(2,1)} async-done(((bf16[1,64,1024]{2,1,0:T(8,128)(2,1)}), bf16[1,1024,1024]{2,1,0:T(8,128)(2,1)}) %all-gather.19.cloned.1.call-update) | async-done | bytes 2097168 | tf_op jit(solution)/shard_map/all_gather | solution.py:52
  225.6 3.0 fusion.10
  228.7 3.7 multiply_convert_fusion.5
  233.3 4.2 %fusion.64 = f32[512,1024]{1,0:T(8,128)} fusion(bf16[512,1024]{1,0:T(8,128)(2,1)S(1)} %multiply_convert_fusion.5, bf16[1024,1024]{1,0:T(8,128)(2,1)} %bitcast_convert_fusion), kind=kOutput, calls=%fused_computation.103 | convolution fusion | flops 1073741824 | bytes 5242880 | tf_op jit(solution)/shard_map/dot_general | solution.py:63
  237.6 2.1 gather_fusion
  239.6 3.4 select_bitcast_fusion
  243.0 4.1 %fusion.61 = (bf16[1024,1024]{1,0:T(8,128)(2,1)}, f32[1024,1024]{1,0:T(8,128)}) fusion(bf16[512,1024]{1,0:T(8,128)(2,1)S(1)} %copy-done.20, f32[512,1024]{1,0:T(8,128)S(1)} %copy-done.8), kind=kOutput, calls=%fused_computation.102 | convolution fusion | flops 1077411840 | bytes 9437184 | tf_op jit(solution)/shard_map/dot_general | solution.py:67
  248.6 86.0 %all-reduce.2.cloned.1.call-done = f32[512,1024]{1,0:T(8,128)} async-done(((f32[512,1024]{1,0:T(8,128)}), f32[512,1024]{1,0:T(8,128)}) %all-reduce.2.cloned.1.call-update) | async-done | bytes 2097168 | tf_op jit(solution)/shard_map/psum | solution.py:66
  334.6 3.0 multiply_convert_fusion.4
  337.5 4.0 %multiply_convert_fusion.3 = bf16[512,1024]{1,0:T(8,128)(2,1)S(1)} fusion(f32[512,1024]{1,0:T(8,128)} %get-tuple-element.21, bf16[512,1024]{1,0:T(8,128)(2,1)S(1)} %multiply_convert_fusion.4, bf16[1,1024,1024]{2,1,0:T(8,128)(2,1)} %all-gather.19.cloned.1.call-done), kind=kOutput, calls=%fused_computation.40 | convolution fusion | flops 1078460416 | bytes 6291456 | tf_op jit(solution)/shard_map/dot_general | solution.py:77
  344.1 2.6 multiply_convert_fusion.1
  346.7 4.3 %bitcast_dynamic-update-slice_fusion.4 = (f32[5,64,1024]{2,1,0:T(8,128)S(1)}, bf16[64,1024]{1,0:T(8,128)(2,1)S(1)}) fusion(f32[512,1024]{1,0:T(8,128)} %get-tuple-element.15, bf16[512,1024]{1,0:T(8,128)(2,1)} %multiply_convert_fusion.1, bf16[1,1024,1024]{2,1,0:T(8,128)(2,1)} %all-gather.13.cloned.1.call-done, bf16[512,1024]{1,0:T(8,128)(2,1)S(1)} %copy-done, ...), kind=kOutput, calls=%fused_computation.72 | convolution fusion | flops 1145634816 | bytes 5767172 | tf_op jit(solution)/shard_map/dot_general | solution.py:73
  351.1 1.8 bitcast_dynamic-update-slice_fusion.3
  355.5 1.7 bitcast_dynamic-update-slice_fusion.2
  360.2 1.8 collective-permute-done.5
  364.6 4.2 %collective-permute-done.7 = bf16[64,1024]{1,0:T(8,128)(2,1)S(1)} collective-permute-done((bf16[64,1024]{1,0:T(8,128)(2,1)S(1)}, bf16[64,1024]{1,0:T(8,128)(2,1)S(1)}, u32[]{:S(2)}, u32[]{:S(2)}) %collective-permute-start.7) | collective-permute-done | bytes 131104 | tf_op jit(solution)/shard_map/ppermute | solution.py:42
  370.2 5.4 %collective-permute-done.9 = bf16[64,1024]{1,0:T(8,128)(2,1)S(1)} collective-permute-done((bf16[64,1024]{1,0:T(8,128)(2,1)S(1)}, bf16[64,1024]{1,0:T(8,128)(2,1)S(1)}, u32[]{:S(2)}, u32[]{:S(2)}) %collective-permute-start.9) | collective-permute-done | bytes 131104 | tf_op jit(solution)/shard_map/ppermute | solution.py:42
  378.4 5.3 %fusion.1 = f32[1,1024,1024]{2,1,0:T(8,128)} fusion(f32[1024,1024]{1,0:T(8,128)S(1)} %copy-done.5, f32[1,1024,1024]{2,1,0:T(8,128)S(1)} %copy-done.3, bf16[1024,1024]{1,0:T(8,128)(2,1)} %collective-permute-done.3, bf16[1024,1024]{1,0:T(8,128)(2,1)} %collective-permute-done.4, pred[]{:T(512)S(6)} %eq.4), kind=kLoop, calls=%fused_computation.4 | loop fusion | flops 9437184 | bytes 16777216 | tf_op jit(solution)/shard_map/broadcast_in_dim | solution.py:117
  (90 shorter events, 25.7 us)
Async XLA Ops:
  7.2 48.7 %copy-start = (bf16[512,1024]{1,0:T(8,128)(2,1)S(1)}, bf16[512,1024]{1,0:T(8,128)(2,1)}, u32[]{:S(2)}) copy-start(bf16[512,1024]{1,0:T(8,128)(2,1)} %param.10) | copy-start | bytes 3145732
  7.2 48.7 %all-gather.11.cloned.1.call-start = ((), (), s32[]{:S(2)}) async-start(), calls=%async_computation.1 | async-start | bytes 2228224 | tf_op jit(solution)/shard_map/all_gather | solution.py:52
  10.4 87.8 %all-gather.13.cloned.1.call-start = ((), (), s32[]{:S(2)}) async-start(), calls=%async_computation.2 | async-start | bytes 2228224 | tf_op jit(solution)/shard_map/all_gather | solution.py:52
  11.2 129.5 %all-gather.15.cloned.1.call-start = ((), (), s32[]{:S(2)}) async-start(), calls=%async_computation.3 | async-start | bytes 2228224 | tf_op jit(solution)/shard_map/all_gather | solution.py:52
  11.9 170.9 %all-gather.17.cloned.1.call-start = ((), (), s32[]{:S(2)}) async-start(), calls=%async_computation.4 | async-start | bytes 2228224 | tf_op jit(solution)/shard_map/all_gather | solution.py:52
  12.5 213.2 %all-gather.19.cloned.1.call-start = ((), (), s32[]{:S(2)}) async-start(), calls=%async_computation.5 | async-start | bytes 2228224 | tf_op jit(solution)/shard_map/all_gather | solution.py:52
  13.1 12.7 %copy-start.1 = (f32[1,512,1024]{2,1,0:T(8,128)S(1)}, f32[1,512,1024]{2,1,0:T(8,128)}, u32[]{:S(2)}) copy-start(f32[1,512,1024]{2,1,0:T(8,128)} %param.7) | copy-start | bytes 6291460
  13.1 12.7 %copy-start.12 = (f32[1024]{0:T(1024)S(1)}, f32[1024]{0:T(1024)}, u32[]{:S(2)}) copy-start(f32[1024]{0:T(1024)} %param.8) | copy-start | bytes 12292
  13.1 321.5 %all-reduce.2.cloned.1.call-start = ((), (), s32[]{:S(2)}) async-start(), calls=%async_computation | async-start | bytes 4194304 | tf_op jit(solution)/shard_map/psum | solution.py:66
  13.1 362.6 %collective-permute-start.10 = (bf16[5,64,1024]{2,1,0:T(8,128)(2,1)}, bf16[5,64,1024]{2,1,0:T(8,128)(2,1)}, u32[]{:S(2)}, u32[]{:S(2)}) collective-permute-start(bf16[5,64,1024]{2,1,0:T(8,128)(2,1)} %copy-done.6), channel_id=1, source_target_pairs={{0,16},{1,17},{2,18},{3,19},{4,20},{5,21},{6,22},{7,23},{8,24},{9,... | collective-permute-start | bytes 1966088 | tf_op jit(solution)/shard_map/ppermute | solution.py:38
  23.0 7.4 %copy-start.15 = (s32[512]{0:T(512)S(1)}, s32[512]{0:T(512)}, u32[]{:S(2)}) copy-start(s32[512]{0:T(512)} %param.11) | copy-start | bytes 6148
  23.0 354.3 %collective-permute-start.4 = (bf16[1024,1024]{1,0:T(8,128)(2,1)}, bf16[1024,1024]{1,0:T(8,128)(2,1)}, u32[]{:S(2)}, u32[]{:S(2)}) collective-permute-start(bf16[1024,1024]{1,0:T(8,128)(2,1)} %bitcast_convert_fusion), channel_id=1, source_target_pairs={{0,16},{1,17},{2,18},{3,19},{4,20},{5,21},{6,22},{7,23},{8,24},{9,... | collective-permute-start | bytes 6291464 | tf_op jit(solution)/shard_map/ppermute | solution.py:38
  25.9 9.9 %collective-permute-start = (f32[513,1]{1,0:T(8,128)S(1)}, f32[513,1]{1,0:T(8,128)S(1)}, u32[]{:S(2)}, u32[]{:S(2)}) collective-permute-start(f32[513,1]{1,0:T(8,128)S(1)} %get-tuple-element.7), channel_id=1, source_target_pairs={{0,1},{1,2},{2,3},{3,4},{4,5},{5,6},{6,7},{7,8},{8,9},{9,10},{10,1... | collective-permute-start | bytes 6164 | tf_op jit(solution)/shard_map/ppermute | solution.py:16
  26.0 10.0 %collective-permute-start.1 = (f32[513,1]{1,0:T(8,128)S(1)}, f32[513,1]{1,0:T(8,128)S(1)}, u32[]{:S(2)}, u32[]{:S(2)}) collective-permute-start(f32[513,1]{1,0:T(8,128)S(1)} %get-tuple-element.8), channel_id=1, source_target_pairs={{1,0},{2,1},{3,2},{4,3},{5,4},{6,5},{7,6},{8,7},{9,8},{10,9},{11,1... | collective-permute-start | bytes 6164 | tf_op jit(solution)/shard_map/ppermute | solution.py:17
  39.1 198.5 %collective-permute-start.2 = (bf16[512,1024]{1,0:T(8,128)(2,1)}, bf16[512,1024]{1,0:T(8,128)(2,1)S(1)}, u32[]{:S(2)}, u32[]{:S(2)}) collective-permute-start(bf16[512,1024]{1,0:T(8,128)(2,1)} %get-tuple-element.5), channel_id=1, source_target_pairs={{0,16},{1,17},{2,18},{3,19},{4,20},{5,21},{6,22},{7,23},{8,24},{9,... | collective-permute-start | bytes 3145736 | tf_op jit(solution)/shard_map/ppermute | solution.py:38
  102.9 42.4 %copy-start.13 = (bf16[512,1024]{1,0:T(8,128)(2,1)}, bf16[512,1024]{1,0:T(8,128)(2,1)S(1)}, u32[]{:S(2)}) copy-start(bf16[512,1024]{1,0:T(8,128)(2,1)S(1)} %get-tuple-element.16) | copy-start | bytes 3145732
  187.5 41.1 %copy-start.14 = (bf16[512,1024]{1,0:T(8,128)(2,1)}, bf16[512,1024]{1,0:T(8,128)(2,1)S(1)}, u32[]{:S(2)}) copy-start(bf16[512,1024]{1,0:T(8,128)(2,1)S(1)} %get-tuple-element.20) | copy-start | bytes 3145732
  228.6 3.7 copy-start.7
  239.6 3.4 copy-start.8
  239.6 3.4 copy-start.20
  247.1 130.3 %collective-permute-start.3 = (bf16[1024,1024]{1,0:T(8,128)(2,1)}, bf16[1024,1024]{1,0:T(8,128)(2,1)}, u32[]{:S(2)}, u32[]{:S(2)}) collective-permute-start(bf16[1024,1024]{1,0:T(8,128)(2,1)} %get-tuple-element.22), channel_id=1, source_target_pairs={{16,0},{17,1},{18,2},{19,3},{20,4},{21,5},{22,6},{23,7},{24,8},{25... | collective-permute-start | bytes 6291464 | tf_op jit(solution)/shard_map/ppermute | solution.py:42
  337.5 4.0 %copy-start.18 = (bf16[1,1024,1024]{2,1,0:T(8,128)(2,1)S(1)}, bf16[1,1024,1024]{2,1,0:T(8,128)(2,1)}, u32[]{:S(2)}) copy-start(bf16[1,1024,1024]{2,1,0:T(8,128)(2,1)} %all-gather.17.cloned.1.call-done) | copy-start | bytes 6291460
  337.5 4.0 %copy-start.22 = (f32[512,1024]{1,0:T(8,128)S(1)}, f32[512,1024]{1,0:T(8,128)}, u32[]{:S(2)}) copy-start(f32[512,1024]{1,0:T(8,128)} %get-tuple-element.19) | copy-start | bytes 6291460
  343.2 3.5 copy-start.11
  351.1 6.1 %copy-start.10 = (bf16[512,1024]{1,0:T(8,128)(2,1)S(1)}, bf16[512,1024]{1,0:T(8,128)(2,1)}, u32[]{:S(2)}) copy-start(bf16[512,1024]{1,0:T(8,128)(2,1)} %copy-done.9) | copy-start | bytes 3145732
  352.9 10.4 %collective-permute-start.6 = (bf16[64,1024]{1,0:T(8,128)(2,1)S(1)}, bf16[64,1024]{1,0:T(8,128)(2,1)S(1)}, u32[]{:S(2)}, u32[]{:S(2)}) collective-permute-start(bf16[64,1024]{1,0:T(8,128)(2,1)S(1)} %get-tuple-element.27), channel_id=1, source_target_pairs={{16,0},{17,1},{18,2},{19,3},{20,4},{21,5},{22,6},{23,7},{24,8},{25... | collective-permute-start | bytes 393224 | tf_op jit(solution)/shard_map/ppermute | solution.py:42
  354.2 7.8 %collective-permute-start.5 = (bf16[64,1024]{1,0:T(8,128)(2,1)S(1)}, bf16[64,1024]{1,0:T(8,128)(2,1)S(1)}, u32[]{:S(2)}, u32[]{:S(2)}) collective-permute-start(bf16[64,1024]{1,0:T(8,128)(2,1)S(1)} %get-tuple-element.25), channel_id=1, source_target_pairs={{16,0},{17,1},{18,2},{19,3},{20,4},{21,5},{22,6},{23,7},{24,8},{25... | collective-permute-start | bytes 393224 | tf_op jit(solution)/shard_map/ppermute | solution.py:42
  357.2 18.5 %copy-start.4 = (f32[1,5,64,1024]{3,2,1,0:T(8,128)S(1)}, f32[1,5,64,1024]{3,2,1,0:T(8,128)}, u32[]{:S(2)}) copy-start(f32[1,5,64,1024]{3,2,1,0:T(8,128)} %param.13) | copy-start | bytes 3932164
  357.2 20.1 %copy-start.5 = (f32[1024,1024]{1,0:T(8,128)S(1)}, f32[1024,1024]{1,0:T(8,128)}, u32[]{:S(2)}) copy-start(f32[1024,1024]{1,0:T(8,128)} %get-tuple-element.23) | copy-start | bytes 12582916
  362.0 6.8 %collective-permute-start.7 = (bf16[64,1024]{1,0:T(8,128)(2,1)S(1)}, bf16[64,1024]{1,0:T(8,128)(2,1)S(1)}, u32[]{:S(2)}, u32[]{:S(2)}) collective-permute-start(bf16[64,1024]{1,0:T(8,128)(2,1)S(1)} %get-tuple-element.29), channel_id=1, source_target_pairs={{16,0},{17,1},{18,2},{19,3},{20,4},{21,5},{22,6},{23,7},{24,8},{25... | collective-permute-start | bytes 393224 | tf_op jit(solution)/shard_map/ppermute | solution.py:42
  363.3 6.9 %collective-permute-start.8 = (bf16[64,1024]{1,0:T(8,128)(2,1)S(1)}, bf16[64,1024]{1,0:T(8,128)(2,1)S(1)}, u32[]{:S(2)}, u32[]{:S(2)}) collective-permute-start(bf16[64,1024]{1,0:T(8,128)(2,1)S(1)} %get-tuple-element.31), channel_id=1, source_target_pairs={{16,0},{17,1},{18,2},{19,3},{20,4},{21,5},{22,6},{23,7},{24,8},{25... | collective-permute-start | bytes 393224 | tf_op jit(solution)/shard_map/ppermute | solution.py:42
  368.8 6.8 %collective-permute-start.9 = (bf16[64,1024]{1,0:T(8,128)(2,1)S(1)}, bf16[64,1024]{1,0:T(8,128)(2,1)S(1)}, u32[]{:S(2)}, u32[]{:S(2)}) collective-permute-start(bf16[64,1024]{1,0:T(8,128)(2,1)S(1)} %get-tuple-element.33), channel_id=1, source_target_pairs={{16,0},{17,1},{18,2},{19,3},{20,4},{21,5},{22,6},{23,7},{24,8},{25... | collective-permute-start | bytes 393224 | tf_op jit(solution)/shard_map/ppermute | solution.py:42
  (8 other events, 14.4 us)
Sparse Core Ops, SparseCore 0:
  10.5 45.2 all-gather.10
  58.0 40.1 all-gather.12
  100.4 40.1 all-gather.14
  142.6 40.1 all-gather.16
  185.4 40.1 all-gather.18
  237.6 96.8 all-reduce.1
where the time goes:
time: 391 us
  waiting for transfers between devices  272 us (70%)
  matrix products  52.6 us (13%)
  starting transfers between devices  22.9 us (6%)
  other arithmetic  22 us (6%)
  between operations  14.6 us (4%)
  local copies, waits for them, and re-layouts  6.81 us (2%)
    all_gather x5, waiting for transfers between devices, plain_training(): lax.all_gather(hidden_narrow[i], 'tile', axis=0, tiled=True)  166 us
    psum x1, waiting for transfers between devices, plain_training(): upstream = lax.psum(partial_grad, 'tile')  86 us
    dot_general x5, matrix products, plain_training(): jnp.dot(activation, full_hidden[i], preferred_element_type=jnp.float32)  21.8 us
    ppermute x6, waiting for transfers between devices, to_solver(): return lax.ppermute(value.astype(jnp.bfloat16), 'role', [(1, 0)])  11.5 us
    dot_general x5, matrix products, plain_training(): gradient = jnp.dot(own_inputs.T, slope, preferred_element_type=jnp.float32)  10.8 us
    broadcast_in_dim x3, other arithmetic, body(): return (fields_next[None], out_next[None], hidden_next[None])  10.3 us
    ppermute x3, starting transfers between devices, to_trainer(): return lax.ppermute(value.astype(jnp.bfloat16), 'role', [(0, 1)])  10.2 us
    dot_general x3, matrix products, plain_training(): lax.dot_general(slope, full_hidden[i], (((1,), (1,)), ((), ())), preferre...  8.2 us
  transfers between devices with their start and end apart: 17, of which 11 were waited for; matrix products, arithmetic and copies ran while one was open for 18% of the time, Pallas kernels for 0%

commit v1 on v0

--- a/solution.py
+++ b/solution.py
@@ -63,7 +63,20 @@
     partial_grad = lax.dot_general(
         residual, out_narrow, (((1,), (1,)), ((), ())), preferred_element_type=jnp.float32
     )
-    upstream = lax.psum(partial_grad, "tile")
+
+    def turn_pairs_all(incoming_x):
+        a_name = "tile"
+        n_chips = jax.lax.psum(1, a_name)
+        inter, part_next = (incoming_x, 0)
+        while 1 << part_next < n_chips:
+            x_now = jax.lax.ppermute(
+                inter, a_name, [(i0, i0 ^ 1 << part_next) for i0 in range(n_chips)]
+            )
+            inter = inter + x_now
+            part_next = part_next + 1
+        return inter
+
+    upstream = turn_pairs_all(partial_grad)
     grad_out = jnp.dot(activation.T, residual, preferred_element_type=jnp.float32)
     sent_out = to_solver(grad_out)
     gradients, sent = ([], [])

time: 391 us -> 475 us (1.21)
  waiting for transfers between devices: 272 us -> 353 us
  matrix products: 52.6 us -> 47.4 us
    ppermute x0 -> x4, waiting for transfers between devices: none -> 100 us  [turn_pairs_all(): jax.lax.ppermute(inter, a_name, [(i0, i0 ^ 1 << part_next) for i0 in rang...]
    psum x1 -> x0, waiting for transfers between devices: 86 us -> none  [plain_training(): upstream = lax.psum(partial_grad, 'tile')]
    ppermute x1, waiting for transfers between devices: 5.41 us -> 40.6 us  [extended(): before = lax.ppermute(last, axis, up)]
    all_gather x5, waiting for transfers between devices: 166 us -> 191 us  [plain_training(): lax.all_gather(hidden_narrow[i], 'tile', axis=0, tiled=True)]
    ppermute x3, waiting for transfers between devices: 0.01 us -> 11 us  [to_trainer(): return lax.ppermute(value.astype(jnp.bfloat16), 'role', [(0, 1)])]
  transfers between devices with their start and end apart: 17 -> 20, of which waited for: 11 -> 14; matrix products, arithmetic and copies ran while one was open for 18% -> 13% of each run, Pallas kernels for 0% -> 0%
where the time goes in v1:
time: 475 us; the launch traced here: 473 us
  waiting for transfers between devices  353 us (74%)
  matrix products  47.4 us (10%)
  other arithmetic  26.7 us (6%)
  starting transfers between devices  26.5 us (6%)
  between operations  14.2 us (3%)
  local copies, waits for them, and re-layouts  5.25 us (1%)
    all_gather x5, waiting for transfers between devices, plain_training(): lax.all_gather(hidden_narrow[i], 'tile', axis=0, tiled=True)  191 us
    ppermute x4, waiting for transfers between devices, turn_pairs_all(): jax.lax.ppermute(inter, a_name, [(i0, i0 ^ 1 << part_next) for i0 in rang...  100 us
    ppermute x1, waiting for transfers between devices, extended(): before = lax.ppermute(last, axis, up)  40.6 us
    dot_general x5, matrix products, plain_training(): jnp.dot(activation, full_hidden[i], preferred_element_type=jnp.float32)  20.4 us
    ppermute x3, starting transfers between devices, to_trainer(): return lax.ppermute(value.astype(jnp.bfloat16), 'role', [(0, 1)])  13 us
    broadcast_in_dim x3, other arithmetic, body(): return (fields_next[None], out_next[None], hidden_next[None])  11.6 us
    ppermute x3, waiting for transfers between devices, to_trainer(): return lax.ppermute(value.astype(jnp.bfloat16), 'role', [(0, 1)])  11 us
    dot_general x5, matrix products, plain_training(): gradient = jnp.dot(own_inputs.T, slope, preferred_element_type=jnp.float32)  10.5 us
  transfers between devices with their start and end apart: 20, of which 14 were waited for; matrix products, arithmetic and copies ran while one was open for 13% of the time, Pallas kernels for 0%

profile of v1, /device:TPU:0, one launch (start us, length us, event | category | flops | bytes accessed | tf_op | source)
XLA Modules:
  0.0 473.2 jit_solution(4574734170872293664)
XLA Ops:
  7.2 2.3 bitcast_convert_fusion.1
  14.2 3.8 bitcast_convert_fusion
  18.0 37.9 %all-gather.11.cloned.1.call-done = bf16[1,1024,1024]{2,1,0:T(8,128)(2,1)} async-done(((bf16[1,64,1024]{2,1,0:T(8,128)(2,1)}), bf16[1,1024,1024]{2,1,0:T(8,128)(2,1)}) %all-gather.11.cloned.1.call-update) | async-done | bytes 2097168 | tf_op jit(solution)/shard_map/all_gather | solution.py:52
  55.9 4.4 multiply_convert_fusion.10
  60.3 38.0 %all-gather.13.cloned.1.call-done = bf16[1,1024,1024]{2,1,0:T(8,128)(2,1)} async-done(((bf16[1,64,1024]{2,1,0:T(8,128)(2,1)}), bf16[1,1024,1024]{2,1,0:T(8,128)(2,1)}) %all-gather.13.cloned.1.call-update) | async-done | bytes 2097168 | tf_op jit(solution)/shard_map/all_gather | solution.py:52
  98.3 4.4 multiply_convert_fusion.9
  102.7 38.5 %all-gather.15.cloned.1.call-done = bf16[1,1024,1024]{2,1,0:T(8,128)(2,1)} async-done(((bf16[1,64,1024]{2,1,0:T(8,128)(2,1)}), bf16[1,1024,1024]{2,1,0:T(8,128)(2,1)}) %all-gather.15.cloned.1.call-update) | async-done | bytes 2097168 | tf_op jit(solution)/shard_map/all_gather | solution.py:52
  141.2 4.3 multiply_convert_fusion.8
  145.5 38.5 %all-gather.17.cloned.1.call-done = bf16[1,1024,1024]{2,1,0:T(8,128)(2,1)} async-done(((bf16[1,64,1024]{2,1,0:T(8,128)(2,1)}), bf16[1,1024,1024]{2,1,0:T(8,128)(2,1)}) %all-gather.17.cloned.1.call-update) | async-done | bytes 2097168 | tf_op jit(solution)/shard_map/all_gather | solution.py:52
  184.0 4.4 multiply_convert_fusion.7
  188.4 38.4 %all-gather.19.cloned.1.call-done = bf16[1,1024,1024]{2,1,0:T(8,128)(2,1)} async-done(((bf16[1,64,1024]{2,1,0:T(8,128)(2,1)}), bf16[1,1024,1024]{2,1,0:T(8,128)(2,1)}) %all-gather.19.cloned.1.call-update) | async-done | bytes 2097168 | tf_op jit(solution)/shard_map/all_gather | solution.py:52
  226.8 3.0 fusion.10
  229.8 3.7 multiply_convert_fusion.5
  233.5 2.9 fusion.64
  236.7 3.9 collective-permute-done.5
  241.7 47.2 %collective-permute-done.6 = f32[512,1024]{1,0:T(8,128)S(1)} collective-permute-done((f32[512,1024]{1,0:T(8,128)S(1)}, f32[512,1024]{1,0:T(8,128)S(1)}, u32[]{:S(2)}, u32[]{:S(2)}) %collective-permute-start.6) | collective-permute-done | bytes 2097184 | tf_op jit(solution)/shard_map/ppermute | solution.py:72
  289.9 4.8 %collective-permute-start.4 = (bf16[1024,1024]{1,0:T(8,128)(2,1)}, bf16[1024,1024]{1,0:T(8,128)(2,1)}, u32[]{:S(2)}, u32[]{:S(2)}) collective-permute-start(bf16[1024,1024]{1,0:T(8,128)(2,1)} %bitcast_convert_fusion), channel_id=1, source_target_pairs={{0,16},{1,17},{2,18},{3,19},{4,20},{5,21},{6,22},{7,23},{8,24},{9,... | collective-permute-start | bytes 6291464 | tf_op jit(solution)/shard_map/ppermute | solution.py:38
  294.7 4.1 collective-permute-start.1
  298.8 40.6 %collective-permute-done = f32[513,1]{1,0:T(8,128)S(1)} collective-permute-done((f32[513,1]{1,0:T(8,128)S(1)}, f32[513,1]{1,0:T(8,128)S(1)}, u32[]{:S(2)}, u32[]{:S(2)}) %collective-permute-start) | collective-permute-done | bytes 2084 | tf_op jit(solution)/shard_map/ppermute | solution.py:16
  339.6 4.0 fusion.61
  345.6 2.0 fusion.59
  347.7 6.1 %collective-permute-start.2 = (bf16[512,1024]{1,0:T(8,128)(2,1)S(1)}, bf16[512,1024]{1,0:T(8,128)(2,1)S(1)}, u32[]{:S(2)}, u32[]{:S(2)}) collective-permute-start(bf16[512,1024]{1,0:T(8,128)(2,1)S(1)} %get-tuple-element.5), channel_id=1, source_target_pairs={{0,16},{1,17},{2,18},{3,19},{4,20},{5,21},{6,22},{7,23},{8,24},{9,... | collective-permute-start | bytes 3145736 | tf_op jit(solution)/shard_map/ppermute | solution.py:38
  355.6 2.2 collective-permute-start.14
  357.8 11.0 %collective-permute-done.2 = bf16[512,1024]{1,0:T(8,128)(2,1)S(1)} collective-permute-done((bf16[512,1024]{1,0:T(8,128)(2,1)S(1)}, bf16[512,1024]{1,0:T(8,128)(2,1)S(1)}, u32[]{:S(2)}, u32[]{:S(2)}) %collective-permute-start.2) | collective-permute-done | bytes 1048608 | tf_op jit(solution)/shard_map/ppermute | solution.py:38
  368.7 2.0 gather_fusion
  370.8 3.4 select_bitcast_fusion
  374.2 6.7 %fusion.1 = f32[1,1024,1024]{2,1,0:T(8,128)} fusion(f32[1024,1024]{1,0:T(8,128)} %get-tuple-element.23, f32[1,1024,1024]{2,1,0:T(8,128)S(1)} %copy-done.2, bf16[1024,1024]{1,0:T(8,128)(2,1)} %collective-permute-done.3, bf16[1024,1024]{1,0:T(8,128)(2,1)} %collective-permute-done.4, pred[]{:T(512)S(6)} %eq.4), kind=kLoop, calls=%fused_computation.4 | loop fusion | flops 9437184 | bytes 16777216 | tf_op jit(solution)/shard_map/broadcast_in_dim | solution.py:130
  380.8 49.2 %collective-permute-done.8 = f32[512,1024]{1,0:T(8,128)} collective-permute-done((f32[512,1024]{1,0:T(8,128)}, f32[512,1024]{1,0:T(8,128)}, u32[]{:S(2)}, u32[]{:S(2)}) %collective-permute-start.8) | collective-permute-done | bytes 2097184 | tf_op jit(solution)/shard_map/ppermute | solution.py:72
  430.0 3.3 multiply_convert_fusion.4
  437.8 2.6 multiply_convert_fusion.1
  440.4 4.3 bitcast_dynamic-update-slice_fusion.4
  460.4 2.8 collective-permute-done.12
  (96 shorter events, 34.4 us)
Async XLA Ops:
  7.2 48.7 %copy-start = (bf16[512,1024]{1,0:T(8,128)(2,1)S(1)}, bf16[512,1024]{1,0:T(8,128)(2,1)}, u32[]{:S(2)}) copy-start(bf16[512,1024]{1,0:T(8,128)(2,1)} %param.10) | copy-start | bytes 3145732
  7.2 48.7 %all-gather.11.cloned.1.call-start = ((), (), s32[]{:S(2)}) async-start(), calls=%async_computation | async-start | bytes 2228224 | tf_op jit(solution)/shard_map/all_gather | solution.py:52
  11.6 86.7 %all-gather.13.cloned.1.call-start = ((), (), s32[]{:S(2)}) async-start(), calls=%async_computation.1 | async-start | bytes 2228224 | tf_op jit(solution)/shard_map/all_gather | solution.py:52
  12.3 128.9 %all-gather.15.cloned.1.call-start = ((), (), s32[]{:S(2)}) async-start(), calls=%async_computation.2 | async-start | bytes 2228224 | tf_op jit(solution)/shard_map/all_gather | solution.py:52
  13.1 171.0 %all-gather.17.cloned.1.call-start = ((), (), s32[]{:S(2)}) async-start(), calls=%async_computation.3 | async-start | bytes 2228224 | tf_op jit(solution)/shard_map/all_gather | solution.py:52
  13.6 213.2 %all-gather.19.cloned.1.call-start = ((), (), s32[]{:S(2)}) async-start(), calls=%async_computation.4 | async-start | bytes 2228224 | tf_op jit(solution)/shard_map/all_gather | solution.py:52
  60.3 42.4 %copy-start.13 = (bf16[512,1024]{1,0:T(8,128)(2,1)}, bf16[512,1024]{1,0:T(8,128)(2,1)S(1)}, u32[]{:S(2)}) copy-start(bf16[512,1024]{1,0:T(8,128)(2,1)S(1)} %get-tuple-element.14) | copy-start | bytes 3145732
  102.7 42.8 %copy-start.12 = (bf16[512,1024]{1,0:T(8,128)(2,1)}, bf16[512,1024]{1,0:T(8,128)(2,1)S(1)}, u32[]{:S(2)}) copy-start(bf16[512,1024]{1,0:T(8,128)(2,1)S(1)} %get-tuple-element.16) | copy-start | bytes 3145732
  145.5 42.9 %copy-start.11 = (bf16[512,1024]{1,0:T(8,128)(2,1)}, bf16[512,1024]{1,0:T(8,128)(2,1)S(1)}, u32[]{:S(2)}) copy-start(bf16[512,1024]{1,0:T(8,128)(2,1)S(1)} %get-tuple-element.18) | copy-start | bytes 3145732
  188.4 41.4 %copy-start.10 = (bf16[512,1024]{1,0:T(8,128)(2,1)}, bf16[512,1024]{1,0:T(8,128)(2,1)S(1)}, u32[]{:S(2)}) copy-start(bf16[512,1024]{1,0:T(8,128)(2,1)S(1)} %get-tuple-element.20) | copy-start | bytes 3145732
  229.8 109.7 %copy-start.4 = (f32[512,1024]{1,0:T(8,128)}, f32[512,1024]{1,0:T(8,128)S(1)}, u32[]{:S(2)}) copy-start(f32[512,1024]{1,0:T(8,128)S(1)} %fusion.10) | copy-start | bytes 6291460
  236.4 4.2 collective-permute-start.5
  241.0 48.7 %copy-start.9 = (f32[1024]{0:T(1024)S(1)}, f32[1024]{0:T(1024)}, u32[]{:S(2)}) copy-start(f32[1024]{0:T(1024)} %param.8) | copy-start | bytes 12292
  241.0 47.8 %collective-permute-start.6 = (f32[512,1024]{1,0:T(8,128)S(1)}, f32[512,1024]{1,0:T(8,128)S(1)}, u32[]{:S(2)}, u32[]{:S(2)}) collective-permute-start(f32[512,1024]{1,0:T(8,128)S(1)} %add.97), channel_id=1, source_target_pairs={{0,2},{1,3},{2,0},{3,1},{4,6},{5,7},{6,4},{7,5},{8,10},{9,11},{10,... | collective-permute-start | bytes 6291464 | tf_op jit(solution)/shard_map/ppermute | solution.py:72
  289.3 64.5 %collective-permute-start.7 = (f32[512,1024]{1,0:T(8,128)S(1)}, f32[512,1024]{1,0:T(8,128)S(1)}, u32[]{:S(2)}, u32[]{:S(2)}) collective-permute-start(f32[512,1024]{1,0:T(8,128)S(1)} %add.98), channel_id=1, source_target_pairs={{0,4},{1,5},{2,6},{3,7},{4,0},{5,1},{6,2},{7,3},{8,12},{9,13},{10,... | collective-permute-start | bytes 6291464 | tf_op jit(solution)/shard_map/ppermute | solution.py:72
  289.9 49.6 %collective-permute-start = (f32[513,1]{1,0:T(8,128)S(1)}, f32[513,1]{1,0:T(8,128)S(1)}, u32[]{:S(2)}, u32[]{:S(2)}) collective-permute-start(f32[513,1]{1,0:T(8,128)S(1)} %get-tuple-element.7), channel_id=1, source_target_pairs={{0,1},{1,2},{2,3},{3,4},{4,5},{5,6},{6,7},{7,8},{8,9},{9,10},{10,1... | collective-permute-start | bytes 6164 | tf_op jit(solution)/shard_map/ppermute | solution.py:16
  289.9 84.2 %collective-permute-start.4 = (bf16[1024,1024]{1,0:T(8,128)(2,1)}, bf16[1024,1024]{1,0:T(8,128)(2,1)}, u32[]{:S(2)}, u32[]{:S(2)}) collective-permute-start(bf16[1024,1024]{1,0:T(8,128)(2,1)} %bitcast_convert_fusion), channel_id=1, source_target_pairs={{0,16},{1,17},{2,18},{3,19},{4,20},{5,21},{6,22},{7,23},{8,24},{9,... | collective-permute-start | bytes 6291464 | tf_op jit(solution)/shard_map/ppermute | solution.py:38
  294.7 50.2 %collective-permute-start.1 = (f32[513,1]{1,0:T(8,128)S(1)}, f32[513,1]{1,0:T(8,128)S(1)}, u32[]{:S(2)}, u32[]{:S(2)}) collective-permute-start(f32[513,1]{1,0:T(8,128)S(1)} %get-tuple-element.8), channel_id=1, source_target_pairs={{1,0},{2,1},{3,2},{4,3},{5,4},{6,5},{7,6},{8,7},{9,8},{10,9},{11,1... | collective-permute-start | bytes 6164 | tf_op jit(solution)/shard_map/ppermute | solution.py:17
  343.6 30.6 %collective-permute-start.3 = (bf16[1024,1024]{1,0:T(8,128)(2,1)}, bf16[1024,1024]{1,0:T(8,128)(2,1)}, u32[]{:S(2)}, u32[]{:S(2)}) collective-permute-start(bf16[1024,1024]{1,0:T(8,128)(2,1)} %get-tuple-element.22), channel_id=1, source_target_pairs={{16,0},{17,1},{18,2},{19,3},{20,4},{21,5},{22,6},{23,7},{24,8},{25... | collective-permute-start | bytes 6291464 | tf_op jit(solution)/shard_map/ppermute | solution.py:42
  347.7 10.1 %copy-start.14 = (s32[512]{0:T(512)S(1)}, s32[512]{0:T(512)}, u32[]{:S(2)}) copy-start(s32[512]{0:T(512)} %param.11) | copy-start | bytes 6148
  347.7 21.1 %collective-permute-start.2 = (bf16[512,1024]{1,0:T(8,128)(2,1)S(1)}, bf16[512,1024]{1,0:T(8,128)(2,1)S(1)}, u32[]{:S(2)}, u32[]{:S(2)}) collective-permute-start(bf16[512,1024]{1,0:T(8,128)(2,1)S(1)} %get-tuple-element.5), channel_id=1, source_target_pairs={{0,16},{1,17},{2,18},{3,19},{4,20},{5,21},{6,22},{7,23},{8,24},{9,... | collective-permute-start | bytes 3145736 | tf_op jit(solution)/shard_map/ppermute | solution.py:38
  355.6 74.5 %collective-permute-start.8 = (f32[512,1024]{1,0:T(8,128)}, f32[512,1024]{1,0:T(8,128)}, u32[]{:S(2)}, u32[]{:S(2)}) collective-permute-start(f32[512,1024]{1,0:T(8,128)} %add.99), channel_id=1, source_target_pairs={{0,8},{1,9},{2,10},{3,11},{4,12},{5,13},{6,14},{7,15},{8,0},{9,1},... | collective-permute-start | bytes 6291464 | tf_op jit(solution)/shard_map/ppermute | solution.py:72
  355.6 109.6 %collective-permute-start.14 = (bf16[5,64,1024]{2,1,0:T(8,128)(2,1)}, bf16[5,64,1024]{2,1,0:T(8,128)(2,1)}, u32[]{:S(2)}, u32[]{:S(2)}) collective-permute-start(bf16[5,64,1024]{2,1,0:T(8,128)(2,1)} %bitcast_convert_fusion.1), channel_id=1, source_target_pairs={{0,16},{1,17},{2,18},{3,19},{4,20},{5,21},{6,22},{7,23},{8,24},{9,... | collective-permute-start | bytes 1966088 | tf_op jit(solution)/shard_map/ppermute | solution.py:38
  374.2 55.9 %copy-start.5 = (f32[512,1024]{1,0:T(8,128)S(1)}, f32[512,1024]{1,0:T(8,128)}, u32[]{:S(2)}) copy-start(f32[512,1024]{1,0:T(8,128)} %copy-done.4) | copy-start | bytes 6291460
  380.8 52.5 %copy-start.18 = (bf16[1,1024,1024]{2,1,0:T(8,128)(2,1)S(1)}, bf16[1,1024,1024]{2,1,0:T(8,128)(2,1)}, u32[]{:S(2)}) copy-start(bf16[1,1024,1024]{2,1,0:T(8,128)(2,1)} %all-gather.19.cloned.1.call-done) | copy-start | bytes 6291460
  380.8 52.5 %copy-start.21 = (f32[512,1024]{1,0:T(8,128)S(1)}, f32[512,1024]{1,0:T(8,128)}, u32[]{:S(2)}) copy-start(f32[512,1024]{1,0:T(8,128)} %get-tuple-element.21) | copy-start | bytes 6291460
  446.5 12.4 %collective-permute-start.10 = (bf16[64,1024]{1,0:T(8,128)(2,1)S(1)}, bf16[64,1024]{1,0:T(8,128)(2,1)S(1)}, u32[]{:S(2)}, u32[]{:S(2)}) collective-permute-start(bf16[64,1024]{1,0:T(8,128)(2,1)S(1)} %get-tuple-element.27), channel_id=1, source_target_pairs={{16,0},{17,1},{18,2},{19,3},{20,4},{21,5},{22,6},{23,7},{24,8},{25... | collective-permute-start | bytes 393224 | tf_op jit(solution)/shard_map/ppermute | solution.py:42
  447.8 9.8 %collective-permute-start.9 = (bf16[64,1024]{1,0:T(8,128)(2,1)S(1)}, bf16[64,1024]{1,0:T(8,128)(2,1)S(1)}, u32[]{:S(2)}, u32[]{:S(2)}) collective-permute-start(bf16[64,1024]{1,0:T(8,128)(2,1)S(1)} %get-tuple-element.25), channel_id=1, source_target_pairs={{16,0},{17,1},{18,2},{19,3},{20,4},{21,5},{22,6},{23,7},{24,8},{25... | collective-permute-start | bytes 393224 | tf_op jit(solution)/shard_map/ppermute | solution.py:42
  450.9 9.6 %collective-permute-start.11 = (bf16[64,1024]{1,0:T(8,128)(2,1)S(1)}, bf16[64,1024]{1,0:T(8,128)(2,1)S(1)}, u32[]{:S(2)}, u32[]{:S(2)}) collective-permute-start(bf16[64,1024]{1,0:T(8,128)(2,1)S(1)} %get-tuple-element.29), channel_id=1, source_target_pairs={{16,0},{17,1},{18,2},{19,3},{20,4},{21,5},{22,6},{23,7},{24,8},{25... | collective-permute-start | bytes 393224 | tf_op jit(solution)/shard_map/ppermute | solution.py:42
  452.2 13.0 %copy-start.3 = (f32[1,5,64,1024]{3,2,1,0:T(8,128)S(1)}, f32[1,5,64,1024]{3,2,1,0:T(8,128)}, u32[]{:S(2)}) copy-start(f32[1,5,64,1024]{3,2,1,0:T(8,128)} %param.13) | copy-start | bytes 3932164
  453.6 9.6 %collective-permute-start.12 = (bf16[64,1024]{1,0:T(8,128)(2,1)S(1)}, bf16[64,1024]{1,0:T(8,128)(2,1)S(1)}, u32[]{:S(2)}, u32[]{:S(2)}) collective-permute-start(bf16[64,1024]{1,0:T(8,128)(2,1)S(1)} %get-tuple-element.31), channel_id=1, source_target_pairs={{16,0},{17,1},{18,2},{19,3},{20,4},{21,5},{22,6},{23,7},{24,8},{25... | collective-permute-start | bytes 393224 | tf_op jit(solution)/shard_map/ppermute | solution.py:42
  457.6 7.5 %collective-permute-start.13 = (bf16[64,1024]{1,0:T(8,128)(2,1)S(1)}, bf16[64,1024]{1,0:T(8,128)(2,1)S(1)}, u32[]{:S(2)}, u32[]{:S(2)}) collective-permute-start(bf16[64,1024]{1,0:T(8,128)(2,1)S(1)} %get-tuple-element.33), channel_id=1, source_target_pairs={{16,0},{17,1},{18,2},{19,3},{20,4},{21,5},{22,6},{23,7},{24,8},{25... | collective-permute-start | bytes 393224 | tf_op jit(solution)/shard_map/ppermute | solution.py:42
  (10 other events, 27.7 us)
Sparse Core Ops, SparseCore 0:
  11.7 44.1 all-gather.10
  58.1 40.1 all-gather.12
  101.0 40.1 all-gather.14
  143.8 40.1 all-gather.16
  186.6 40.1 all-gather.18
